TPU v7x, 32 devices: a whole 2x2x4 slice. The times are simulated.
32 devices in a mesh: section: 4 (over x, core), obs: 8 (over z, y).
Axes of the slice: x: 2, y: 2, z: 4, core: 2. Of those that a mesh axis runs over, the one named last changes fastest.
Arguments:
- predictors: bfloat16 [4, 4, 20, 32768], P('section', None, None, 'obs'), may hold values from -5 to 5
- departures: float32 [4, 4, 32768], P('section', None, 'obs'), may hold values from -30 to 30
- obs_precision: float32 [4, 4, 32768], P('section', None, 'obs'), may hold values from 0.3 to 3
- qc_pass: int32 [4, 4, 32768], P('section', None, 'obs'), may hold values 0 or 1
- block_channel: int32 [4, 4, 256], P('section', None, 'obs'), may hold values from 0 to 2047, as said below
- stream_order: int32 [4], replicated, may hold values from 0 to 3, each once
- prior_coeffs: float32 [4, 20, 2048], P(None, None, 'obs'), may hold values from -1 to 1
- prior_info: float32 [4, 210, 2048], P(None, None, 'obs'), may hold values from -1 to 32, as said below
- memory_factor: float32 [2048], P('obs'), may hold values from 0.5 to 0.98
Outputs:
- coeffs: float32 [4, 4, 20, 2048], P('section', None, None, 'obs')
- information: float32 [4, 4, 210, 2048], P('section', None, None, 'obs')
Inputs may be any that keep to these rules, and one draw needn't show every extreme that they name: `block_channel`: among the 32 row blocks of one index of obs, at most 8 have channels in any one range of the 256 channels from a multiple of 256; in every window and stream one such range holds exactly 8 blocks of every index of obs. `stream_order`: each stream appears once. `prior_info`: for every stream and channel the 210 entries are the upper triangle, row by row, of a symmetric positive definite matrix of order 20.
All inputs are finite; a program needn't handle non-finite values. No bound on the sum of `qc_pass` on one device may be relied on, other than what follows from the above.
Results may differ from a plain program's by a relative error of at most 0.0038.
Values sent between devices are 32-bit elements; how exact they have to be, the bound alone decides.
A program may use at most 64 MiB of HBM per device.

v0:
```python
import jax
import jax.numpy as jnp
import numpy as np
from jax import lax
from jax.sharding import PartitionSpec as P

HUBER_SQ = 9.0
PRIOR_WEIGHT = 64.0


def from_behind(array, axis, by):
    size = lax.axis_size(axis)
    pairs = [(i, i + by) for i in range(size) if 0 <= i + by < size]
    return lax.ppermute(array, axis, pairs)


def upper_positions(dimension):
    return np.array(
        [i * dimension + j for i in range(dimension) for j in range(i, dimension)], dtype=np.int32
    )


def solve_packed(packed, target):
    dimension = target.shape[0]
    placing = {}
    counter = 0
    for i in range(dimension):
        for j in range(i, dimension):
            placing[i, j] = counter
            counter += 1
    factor = [[None] * dimension for i in range(dimension)]
    for j in range(dimension):
        pivot_root = jnp.sqrt(
            packed[placing[j, j]] - sum((factor[j][k] * factor[j][k] for k in range(j)))
        )
        factor[j][j] = pivot_root
        for i in range(j + 1, dimension):
            factor[i][j] = (
                packed[placing[j, i]] - sum((factor[i][k] * factor[j][k] for k in range(j)))
            ) / pivot_root
    forward = []
    for i in range(dimension):
        forward.append(
            (target[i] - sum((factor[i][k] * forward[k] for k in range(i)))) / factor[i][i]
        )
    backward = [None] * dimension
    for i in reversed(range(dimension)):
        backward[i] = (
            forward[i] - sum((factor[k][i] * backward[k] for k in range(i + 1, dimension)))
        ) / factor[i][i]
    return jnp.stack(backward)


def block_terms(predicted, departed, precision, passed, block_coeffs):
    pred_count, row_count = predicted.shape
    block_count = block_coeffs.shape[1]
    block_width = row_count // block_count
    upper_index = upper_positions(pred_count)
    shaped = predicted.reshape(pred_count, block_count, block_width)
    offset = jnp.sum(shaped.astype(jnp.float32) * block_coeffs[:, :, None], axis=0)
    residual = departed.reshape(block_count, block_width) - offset
    scale_row = precision.reshape(block_count, block_width)
    weight = (
        passed.reshape(block_count, block_width).astype(jnp.float32)
        * scale_row
        / (1.0 + scale_row * residual * residual / HUBER_SQ)
    )
    weighted = (weight[None] * shaped.astype(jnp.float32)).astype(jnp.bfloat16)
    chi_square = jnp.sum(weight * residual * residual)
    passed_count = jnp.sum(passed.astype(jnp.float32))
    gram_full = lax.dot_general(
        weighted, shaped, (((2,), (2,)), ((1,), (1,))), preferred_element_type=jnp.float32
    )
    gram_upper = gram_full.reshape(block_count, pred_count * pred_count)[:, upper_index]
    gradient = jnp.sum(weighted.astype(jnp.float32) * residual[None], axis=2).T
    return (jnp.concatenate([gram_upper, gradient], axis=1), jnp.stack([chi_square, passed_count]))


def local(
    predictors,
    departures,
    obs_precision,
    qc_pass,
    block_channel,
    stream_order,
    prior_coeffs,
    prior_info,
    memory_factor,
):
    section_count = lax.axis_size("section")
    obs_devices = lax.axis_size("obs")
    section_place = lax.axis_index("section")
    stream_count = stream_order.shape[0]
    local_channels = memory_factor.shape[0]
    block_count = block_channel.shape[2]
    pred_count = prior_coeffs.shape[1]
    tri_count = prior_info.shape[1]
    column_count = tri_count + pred_count
    capacity = 2 * block_count // obs_devices
    local_line = jnp.arange(local_channels, dtype=jnp.float32)
    owner_line = jnp.arange(obs_devices, dtype=jnp.int32)
    slot_line = jnp.arange(obs_devices * capacity, dtype=jnp.int32)
    highest = lax.Precision.HIGHEST

    def pack_blocks(block_sums, channel):
        owner_index = channel // local_channels
        inner_channel = channel % local_channels
        owner_hot = (owner_index[:, None] == owner_line[None, :]).astype(jnp.int32)
        ranking = jnp.sum((jnp.cumsum(owner_hot, axis=0) - 1) * owner_hot, axis=1)
        slot_of = owner_index * capacity + ranking
        placing = (slot_of[:, None] == slot_line[None, :]).astype(jnp.float32)
        send_rows = lax.dot_general(
            placing,
            block_sums,
            (((0,), (0,)), ((), ())),
            precision=highest,
            preferred_element_type=jnp.float32,
        ).reshape(obs_devices, capacity, column_count)
        send_channel = (
            lax.dot_general(
                placing,
                (inner_channel + 1).astype(jnp.float32),
                (((0,), (0,)), ((), ())),
                precision=highest,
                preferred_element_type=jnp.float32,
            ).reshape(obs_devices, capacity)
            - 1.0
        )
        return (send_rows, send_channel)

    def unpack_blocks(got_rows, got_channel):
        gather_hot = (got_channel.reshape(-1)[:, None] == local_line[None, :]).astype(jnp.float32)
        return lax.dot_general(
            got_rows.reshape(-1, column_count),
            gather_hot,
            (((0,), (0,)), ((), ())),
            precision=highest,
            preferred_element_type=jnp.float32,
        )

    def window_work(state_now, streams):
        beta_prior = state_now[:, :pred_count]
        info_prior = state_now[:, pred_count:]
        all_coeffs = lax.all_gather(beta_prior, "obs", axis=2, tiled=True)
        channel = jnp.take(block_channel[0], streams, axis=0)
        block_coeffs = jax.vmap(lambda coeff_rows, chan: jnp.take(coeff_rows, chan, axis=1))(
            all_coeffs, channel
        )
        block_sums, statistics = jax.vmap(block_terms)(
            jnp.take(predictors[0], streams, axis=0),
            jnp.take(departures[0], streams, axis=0),
            jnp.take(obs_precision[0], streams, axis=0),
            jnp.take(qc_pass[0], streams, axis=0),
            block_coeffs,
        )
        totals = lax.psum(statistics, "obs")
        send_rows, send_channel = jax.vmap(pack_blocks)(block_sums, channel)
        got_rows, got_channel = (
            lax.all_to_all(send_rows, "obs", split_axis=1, concat_axis=1, tiled=True),
            lax.all_to_all(send_channel, "obs", split_axis=1, concat_axis=1, tiled=True),
        )
        normal = jax.vmap(unpack_blocks)(got_rows, got_channel)
        inflation = (totals[:, 0] + PRIOR_WEIGHT) / (totals[:, 1] + PRIOR_WEIGHT)
        info_post = info_prior + normal[:, :tri_count] / inflation[:, None, None]
        beta_post = beta_prior + jax.vmap(solve_packed)(
            info_post, normal[:, tri_count:] / inflation[:, None, None]
        )
        outgoing = jnp.concatenate([beta_post, memory_factor[None, None, :] * info_post], axis=1)
        incoming = from_behind(outgoing, "section", 1)
        return (beta_post, info_post, incoming)

    def fresh_of(streams):
        return jnp.concatenate(
            [jnp.take(prior_coeffs, streams, axis=0), jnp.take(prior_info, streams, axis=0)], axis=1
        )

    coeff_start = jnp.zeros((1, stream_count, pred_count, local_channels), jnp.float32)
    info_start = jnp.zeros((1, stream_count, tri_count, local_channels), jnp.float32)

    def tick_step(t, loop_state):
        incoming, coeff_out, info_out = loop_state
        entry_index = t - section_place
        usable = (entry_index >= 0) & (entry_index < stream_count)
        slot_index = jnp.clip(entry_index, 0, stream_count - 1)
        streams = lax.dynamic_slice_in_dim(stream_order, slot_index, 1, 0)
        state_now = jnp.where(
            (section_place == 0) | jnp.logical_not(usable), fresh_of(streams), incoming
        )
        beta_post, info_post, incoming = window_work(state_now, streams)

        def store_entry(buffer, result):
            current = lax.dynamic_slice_in_dim(buffer, slot_index, 1, 1)
            updated = jnp.where(usable, result[None], current)
            return lax.dynamic_update_slice_in_dim(buffer, updated, slot_index, 1)

        return (incoming, store_entry(coeff_out, beta_post), store_entry(info_out, info_post))

    initial = (jnp.zeros((1, column_count, local_channels), jnp.float32), coeff_start, info_start)
    final_state = lax.fori_loop(0, stream_count + section_count - 1, tick_step, initial)
    return (final_state[1], final_state[2])


def solution(mesh):
    in_specs = (
        P("section", None, None, "obs"),
        P("section", None, "obs"),
        P("section", None, "obs"),
        P("section", None, "obs"),
        P("section", None, "obs"),
        P(),
        P(None, None, "obs"),
        P(None, None, "obs"),
        P("obs"),
    )
    out_specs = (P("section", None, None, "obs"), P("section", None, None, "obs"))
    return jax.shard_map(local, mesh=mesh, in_specs=in_specs, out_specs=out_specs, check_vma=False)
```

profile of v0, /device:TPU:1, one launch (start us, length us, event | category | flops | bytes accessed | tf_op | source)
XLA Modules:
  0.0 688.5 jit_solution(5905409147109336993)
XLA Ops:
  0.6 1.5 copy.675
  2.9 684.6 %while.38 = (s32[]{:T(128)}, f32[1,230,256]{2,1,0:T(8,128)S(1)}, f32[1,4,20,256]{3,1,2,0:T(4,128)S(1)}, f32[1,4,210,256]{3,1,2,0:T(4,128)S(1)}, s32[]{:T(128)}, ...) while((s32[]{:T(128)}, f32[1,230,256]{2,1,0:T(8,128)S(1)}, ...), condition=%wide.region_8.10_spmd.clone.clone, body=%wide.region_0.9_spmd.sunk.clone.clone.sunk | while | flops 57759508 | bytes 13853709 | solution.py:199
  7.5 6.4 all-to-all-start.1
  13.9 1.4 constant_dynamic-slice_fusion.10
  16.3 24.6 %all_gather.15 = f32[1,20,2048]{2,1,0:T(8,128)S(1)} all-gather(f32[1,20,256]{2,1,0:T(8,128)S(1)} %slice.5342), channel_id=1, replica_groups=mesh['section'=4,'obs'=8] {'obs'}, dimensions={2}, use_global_device_ids=true | all-gather | bytes 184320 | tf_op jit(solution)/shard_map/while/body/eval_jaxpr/all_gather | solution.py:144
  42.3 1.6 fusion.473
  47.6 17.5 %psum.19 = f32[1,2]{1,0:T(1,128)S(1)} all-reduce(f32[1,2]{1,0:T(1,128)S(1)} %maximum_bitcast_fusion.6), channel_id=1, replica_groups=mesh['section'=4,'obs'=8] {'obs'}, use_global_device_ids=true, to_apply=%region_7.8 | all-reduce | flops 2 | bytes 16 | tf_op jit(solution)/shard_map/while/body/eval_jaxpr/psum | solution.py:156
  68.0 3.4 all-to-all-start
  72.6 4.4 all-to-all-done
  83.2 15.7 %collective-permute-start = (f32[1,230,256]{2,1,0:T(8,128)S(1)}, f32[1,230,256]{2,1,0:T(8,128)S(1)}, u32[]{:S(2)}, u32[]{:S(2)}) collective-permute-start(f32[1,230,256]{2,1,0:T(8,128)S(1)} %pad_maximum_fusion.2), channel_id=1, source_target_pairs={{0,8},{8,16},{16,24},{1,9},{9,17},{17,25},{2,10},{10,18},{18,26},{... | collective-permute-start | bytes 706568 | tf_op jit(solution)/shard_map/while/body/eval_jaxpr/ppermute | solution.py:14
  99.3 5.9 dynamic_update_slice.31
  109.8 3.3 all-to-all-start.1
  113.2 1.4 constant_dynamic-slice_fusion.10
  115.6 25.2 %all_gather.15 = f32[1,20,2048]{2,1,0:T(8,128)S(1)} all-gather(f32[1,20,256]{2,1,0:T(8,128)S(1)} %slice.5342), channel_id=1, replica_groups=mesh['section'=4,'obs'=8] {'obs'}, dimensions={2}, use_global_device_ids=true | all-gather | bytes 184320 | tf_op jit(solution)/shard_map/while/body/eval_jaxpr/all_gather | solution.py:144
  142.2 1.6 fusion.473
  147.5 17.3 %psum.19 = f32[1,2]{1,0:T(1,128)S(1)} all-reduce(f32[1,2]{1,0:T(1,128)S(1)} %maximum_bitcast_fusion.6), channel_id=1, replica_groups=mesh['section'=4,'obs'=8] {'obs'}, use_global_device_ids=true, to_apply=%region_7.8 | all-reduce | flops 2 | bytes 16 | tf_op jit(solution)/shard_map/while/body/eval_jaxpr/psum | solution.py:156
  167.6 3.4 all-to-all-start
  172.3 4.4 all-to-all-done
  182.9 13.1 %collective-permute-start = (f32[1,230,256]{2,1,0:T(8,128)S(1)}, f32[1,230,256]{2,1,0:T(8,128)S(1)}, u32[]{:S(2)}, u32[]{:S(2)}) collective-permute-start(f32[1,230,256]{2,1,0:T(8,128)S(1)} %pad_maximum_fusion.2), channel_id=1, source_target_pairs={{0,8},{8,16},{16,24},{1,9},{9,17},{17,25},{2,10},{10,18},{18,26},{... | collective-permute-start | bytes 706568 | tf_op jit(solution)/shard_map/while/body/eval_jaxpr/ppermute | solution.py:14
  196.4 5.9 dynamic_update_slice.31
  206.9 3.3 all-to-all-start.1
  210.2 1.4 constant_dynamic-slice_fusion.10
  212.6 24.6 %all_gather.15 = f32[1,20,2048]{2,1,0:T(8,128)S(1)} all-gather(f32[1,20,256]{2,1,0:T(8,128)S(1)} %slice.5342), channel_id=1, replica_groups=mesh['section'=4,'obs'=8] {'obs'}, dimensions={2}, use_global_device_ids=true | all-gather | bytes 184320 | tf_op jit(solution)/shard_map/while/body/eval_jaxpr/all_gather | solution.py:144
  238.7 1.6 fusion.473
  244.0 17.5 %psum.19 = f32[1,2]{1,0:T(1,128)S(1)} all-reduce(f32[1,2]{1,0:T(1,128)S(1)} %maximum_bitcast_fusion.6), channel_id=1, replica_groups=mesh['section'=4,'obs'=8] {'obs'}, use_global_device_ids=true, to_apply=%region_7.8 | all-reduce | flops 2 | bytes 16 | tf_op jit(solution)/shard_map/while/body/eval_jaxpr/psum | solution.py:156
  264.4 3.4 all-to-all-start
  269.0 4.4 all-to-all-done
  279.6 13.4 %collective-permute-start = (f32[1,230,256]{2,1,0:T(8,128)S(1)}, f32[1,230,256]{2,1,0:T(8,128)S(1)}, u32[]{:S(2)}, u32[]{:S(2)}) collective-permute-start(f32[1,230,256]{2,1,0:T(8,128)S(1)} %pad_maximum_fusion.2), channel_id=1, source_target_pairs={{0,8},{8,16},{16,24},{1,9},{9,17},{17,25},{2,10},{10,18},{18,26},{... | collective-permute-start | bytes 706568 | tf_op jit(solution)/shard_map/while/body/eval_jaxpr/ppermute | solution.py:14
  293.4 5.9 dynamic_update_slice.31
  303.9 3.3 all-to-all-start.1
  307.3 1.4 constant_dynamic-slice_fusion.10
  309.7 24.8 %all_gather.15 = f32[1,20,2048]{2,1,0:T(8,128)S(1)} all-gather(f32[1,20,256]{2,1,0:T(8,128)S(1)} %slice.5342), channel_id=1, replica_groups=mesh['section'=4,'obs'=8] {'obs'}, dimensions={2}, use_global_device_ids=true | all-gather | bytes 184320 | tf_op jit(solution)/shard_map/while/body/eval_jaxpr/all_gather | solution.py:144
  336.0 1.6 fusion.473
  341.3 17.6 %psum.19 = f32[1,2]{1,0:T(1,128)S(1)} all-reduce(f32[1,2]{1,0:T(1,128)S(1)} %maximum_bitcast_fusion.6), channel_id=1, replica_groups=mesh['section'=4,'obs'=8] {'obs'}, use_global_device_ids=true, to_apply=%region_7.8 | all-reduce | flops 2 | bytes 16 | tf_op jit(solution)/shard_map/while/body/eval_jaxpr/psum | solution.py:156
  361.8 3.4 all-to-all-start
  366.4 4.4 all-to-all-done
  377.0 13.1 %collective-permute-start = (f32[1,230,256]{2,1,0:T(8,128)S(1)}, f32[1,230,256]{2,1,0:T(8,128)S(1)}, u32[]{:S(2)}, u32[]{:S(2)}) collective-permute-start(f32[1,230,256]{2,1,0:T(8,128)S(1)} %pad_maximum_fusion.2), channel_id=1, source_target_pairs={{0,8},{8,16},{16,24},{1,9},{9,17},{17,25},{2,10},{10,18},{18,26},{... | collective-permute-start | bytes 706568 | tf_op jit(solution)/shard_map/while/body/eval_jaxpr/ppermute | solution.py:14
  390.5 5.9 dynamic_update_slice.31
  401.0 3.3 all-to-all-start.1
  406.7 24.9 %all_gather.15 = f32[1,20,2048]{2,1,0:T(8,128)S(1)} all-gather(f32[1,20,256]{2,1,0:T(8,128)S(1)} %slice.5342), channel_id=1, replica_groups=mesh['section'=4,'obs'=8] {'obs'}, dimensions={2}, use_global_device_ids=true | all-gather | bytes 184320 | tf_op jit(solution)/shard_map/while/body/eval_jaxpr/all_gather | solution.py:144
  433.2 1.6 fusion.473
  438.4 17.2 %psum.19 = f32[1,2]{1,0:T(1,128)S(1)} all-reduce(f32[1,2]{1,0:T(1,128)S(1)} %maximum_bitcast_fusion.6), channel_id=1, replica_groups=mesh['section'=4,'obs'=8] {'obs'}, use_global_device_ids=true, to_apply=%region_7.8 | all-reduce | flops 2 | bytes 16 | tf_op jit(solution)/shard_map/while/body/eval_jaxpr/psum | solution.py:156
  458.5 3.4 all-to-all-start
  463.2 4.4 all-to-all-done
  473.8 13.4 %collective-permute-start = (f32[1,230,256]{2,1,0:T(8,128)S(1)}, f32[1,230,256]{2,1,0:T(8,128)S(1)}, u32[]{:S(2)}, u32[]{:S(2)}) collective-permute-start(f32[1,230,256]{2,1,0:T(8,128)S(1)} %pad_maximum_fusion.2), channel_id=1, source_target_pairs={{0,8},{8,16},{16,24},{1,9},{9,17},{17,25},{2,10},{10,18},{18,26},{... | collective-permute-start | bytes 706568 | tf_op jit(solution)/shard_map/while/body/eval_jaxpr/ppermute | solution.py:14
  487.5 5.9 dynamic_update_slice.31
  498.1 3.3 all-to-all-start.1
  501.4 1.4 constant_dynamic-slice_fusion.10
  503.8 24.8 %all_gather.15 = f32[1,20,2048]{2,1,0:T(8,128)S(1)} all-gather(f32[1,20,256]{2,1,0:T(8,128)S(1)} %slice.5342), channel_id=1, replica_groups=mesh['section'=4,'obs'=8] {'obs'}, dimensions={2}, use_global_device_ids=true | all-gather | bytes 184320 | tf_op jit(solution)/shard_map/while/body/eval_jaxpr/all_gather | solution.py:144
  530.1 1.6 fusion.473
  535.4 17.5 %psum.19 = f32[1,2]{1,0:T(1,128)S(1)} all-reduce(f32[1,2]{1,0:T(1,128)S(1)} %maximum_bitcast_fusion.6), channel_id=1, replica_groups=mesh['section'=4,'obs'=8] {'obs'}, use_global_device_ids=true, to_apply=%region_7.8 | all-reduce | flops 2 | bytes 16 | tf_op jit(solution)/shard_map/while/body/eval_jaxpr/psum | solution.py:156
  555.8 3.4 all-to-all-start
  560.4 4.4 all-to-all-done
  571.0 13.2 %collective-permute-start = (f32[1,230,256]{2,1,0:T(8,128)S(1)}, f32[1,230,256]{2,1,0:T(8,128)S(1)}, u32[]{:S(2)}, u32[]{:S(2)}) collective-permute-start(f32[1,230,256]{2,1,0:T(8,128)S(1)} %pad_maximum_fusion.2), channel_id=1, source_target_pairs={{0,8},{8,16},{16,24},{1,9},{9,17},{17,25},{2,10},{10,18},{18,26},{... | collective-permute-start | bytes 706568 | tf_op jit(solution)/shard_map/while/body/eval_jaxpr/ppermute | solution.py:14
  584.6 5.9 dynamic_update_slice.31
  595.1 3.3 all-to-all-start.1
  598.5 1.4 constant_dynamic-slice_fusion.10
  600.9 24.5 %all_gather.15 = f32[1,20,2048]{2,1,0:T(8,128)S(1)} all-gather(f32[1,20,256]{2,1,0:T(8,128)S(1)} %slice.5342), channel_id=1, replica_groups=mesh['section'=4,'obs'=8] {'obs'}, dimensions={2}, use_global_device_ids=true | all-gather | bytes 184320 | tf_op jit(solution)/shard_map/while/body/eval_jaxpr/all_gather | solution.py:144
  626.8 1.6 fusion.473
  632.1 18.0 %psum.19 = f32[1,2]{1,0:T(1,128)S(1)} all-reduce(f32[1,2]{1,0:T(1,128)S(1)} %maximum_bitcast_fusion.6), channel_id=1, replica_groups=mesh['section'=4,'obs'=8] {'obs'}, use_global_device_ids=true, to_apply=%region_7.8 | all-reduce | flops 2 | bytes 16 | tf_op jit(solution)/shard_map/while/body/eval_jaxpr/psum | solution.py:156
  652.9 3.4 all-to-all-start
  657.6 4.4 all-to-all-done
  668.2 13.1 %collective-permute-start = (f32[1,230,256]{2,1,0:T(8,128)S(1)}, f32[1,230,256]{2,1,0:T(8,128)S(1)}, u32[]{:S(2)}, u32[]{:S(2)}) collective-permute-start(f32[1,230,256]{2,1,0:T(8,128)S(1)} %pad_maximum_fusion.2), channel_id=1, source_target_pairs={{0,8},{8,16},{16,24},{1,9},{9,17},{17,25},{2,10},{10,18},{18,26},{... | collective-permute-start | bytes 706568 | tf_op jit(solution)/shard_map/while/body/eval_jaxpr/ppermute | solution.py:14
  681.7 5.9 dynamic_update_slice.31
  (616 shorter events, 128.2 us)
Async XLA Ops:
  2.2 0.7 copy-start.4
  2.3 0.7 copy-start.5
  2.3 0.7 copy-start.6
  7.5 60.4 %all-to-all-start.1 = ((f32[1,8,8]{2,0,1:T(1,128)}), f32[1,8,8]{2,0,1:T(1,128)S(1)}, u32[]{:S(2)}, u32[]{:S(2)}) async-start(f32[1,8,8]{2,0,1:T(1,128)} %bitcast.2454), calls=%async_computation.1 | async-start | bytes 8192 | tf_op jit(solution)/shard_map/while/body/eval_jaxpr/all_to_all | solution.py:160
  68.0 9.1 %all-to-all-start = ((f32[1,8,8,230]{3,2,0,1:T(8,128)}), f32[1,8,8,230]{3,2,0,1:T(8,128)S(1)}, u32[]{:S(2)}, u32[]{:S(2)}) async-start(f32[1,8,8,230]{3,2,0,1:T(8,128)} %convolution_bitcast_fusion.4), calls=%async_computation | async-start | bytes 131072 | tf_op jit(solution)/shard_map/while/body/eval_jaxpr/all_to_all | solution.py:159
  77.4 0.6 copy-start
  78.8 0.7 slice-start
  80.7 0.7 copy-start.1
  83.2 22.0 %collective-permute-start = (f32[1,230,256]{2,1,0:T(8,128)S(1)}, f32[1,230,256]{2,1,0:T(8,128)S(1)}, u32[]{:S(2)}, u32[]{:S(2)}) collective-permute-start(f32[1,230,256]{2,1,0:T(8,128)S(1)} %pad_maximum_fusion.2), channel_id=1, source_target_pairs={{0,8},{8,16},{16,24},{1,9},{9,17},{17,25},{2,10},{10,18},{18,26},{... | collective-permute-start | bytes 706568 | tf_op jit(solution)/shard_map/while/body/eval_jaxpr/ppermute | solution.py:14
  109.8 57.8 %all-to-all-start.1 = ((f32[1,8,8]{2,0,1:T(1,128)}), f32[1,8,8]{2,0,1:T(1,128)S(1)}, u32[]{:S(2)}, u32[]{:S(2)}) async-start(f32[1,8,8]{2,0,1:T(1,128)} %bitcast.2454), calls=%async_computation.1 | async-start | bytes 8192 | tf_op jit(solution)/shard_map/while/body/eval_jaxpr/all_to_all | solution.py:160
  167.6 9.1 %all-to-all-start = ((f32[1,8,8,230]{3,2,0,1:T(8,128)}), f32[1,8,8,230]{3,2,0,1:T(8,128)S(1)}, u32[]{:S(2)}, u32[]{:S(2)}) async-start(f32[1,8,8,230]{3,2,0,1:T(8,128)} %convolution_bitcast_fusion.4), calls=%async_computation | async-start | bytes 131072 | tf_op jit(solution)/shard_map/while/body/eval_jaxpr/all_to_all | solution.py:159
  177.1 0.6 copy-start
  178.5 0.7 slice-start
  180.4 0.7 copy-start.1
  182.9 19.4 %collective-permute-start = (f32[1,230,256]{2,1,0:T(8,128)S(1)}, f32[1,230,256]{2,1,0:T(8,128)S(1)}, u32[]{:S(2)}, u32[]{:S(2)}) collective-permute-start(f32[1,230,256]{2,1,0:T(8,128)S(1)} %pad_maximum_fusion.2), channel_id=1, source_target_pairs={{0,8},{8,16},{16,24},{1,9},{9,17},{17,25},{2,10},{10,18},{18,26},{... | collective-permute-start | bytes 706568 | tf_op jit(solution)/shard_map/while/body/eval_jaxpr/ppermute | solution.py:14
  206.9 57.5 %all-to-all-start.1 = ((f32[1,8,8]{2,0,1:T(1,128)}), f32[1,8,8]{2,0,1:T(1,128)S(1)}, u32[]{:S(2)}, u32[]{:S(2)}) async-start(f32[1,8,8]{2,0,1:T(1,128)} %bitcast.2454), calls=%async_computation.1 | async-start | bytes 8192 | tf_op jit(solution)/shard_map/while/body/eval_jaxpr/all_to_all | solution.py:160
  264.4 9.1 %all-to-all-start = ((f32[1,8,8,230]{3,2,0,1:T(8,128)}), f32[1,8,8,230]{3,2,0,1:T(8,128)S(1)}, u32[]{:S(2)}, u32[]{:S(2)}) async-start(f32[1,8,8,230]{3,2,0,1:T(8,128)} %convolution_bitcast_fusion.4), calls=%async_computation | async-start | bytes 131072 | tf_op jit(solution)/shard_map/while/body/eval_jaxpr/all_to_all | solution.py:159
  273.8 0.6 copy-start
  275.2 0.7 slice-start
  277.1 0.7 copy-start.1
  279.6 19.7 %collective-permute-start = (f32[1,230,256]{2,1,0:T(8,128)S(1)}, f32[1,230,256]{2,1,0:T(8,128)S(1)}, u32[]{:S(2)}, u32[]{:S(2)}) collective-permute-start(f32[1,230,256]{2,1,0:T(8,128)S(1)} %pad_maximum_fusion.2), channel_id=1, source_target_pairs={{0,8},{8,16},{16,24},{1,9},{9,17},{17,25},{2,10},{10,18},{18,26},{... | collective-permute-start | bytes 706568 | tf_op jit(solution)/shard_map/while/body/eval_jaxpr/ppermute | solution.py:14
  303.9 57.8 %all-to-all-start.1 = ((f32[1,8,8]{2,0,1:T(1,128)}), f32[1,8,8]{2,0,1:T(1,128)S(1)}, u32[]{:S(2)}, u32[]{:S(2)}) async-start(f32[1,8,8]{2,0,1:T(1,128)} %bitcast.2454), calls=%async_computation.1 | async-start | bytes 8192 | tf_op jit(solution)/shard_map/while/body/eval_jaxpr/all_to_all | solution.py:160
  361.8 9.1 %all-to-all-start = ((f32[1,8,8,230]{3,2,0,1:T(8,128)}), f32[1,8,8,230]{3,2,0,1:T(8,128)S(1)}, u32[]{:S(2)}, u32[]{:S(2)}) async-start(f32[1,8,8,230]{3,2,0,1:T(8,128)} %convolution_bitcast_fusion.4), calls=%async_computation | async-start | bytes 131072 | tf_op jit(solution)/shard_map/while/body/eval_jaxpr/all_to_all | solution.py:159
  371.2 0.6 copy-start
  372.6 0.7 slice-start
  374.5 0.7 copy-start.1
  377.0 19.4 %collective-permute-start = (f32[1,230,256]{2,1,0:T(8,128)S(1)}, f32[1,230,256]{2,1,0:T(8,128)S(1)}, u32[]{:S(2)}, u32[]{:S(2)}) collective-permute-start(f32[1,230,256]{2,1,0:T(8,128)S(1)} %pad_maximum_fusion.2), channel_id=1, source_target_pairs={{0,8},{8,16},{16,24},{1,9},{9,17},{17,25},{2,10},{10,18},{18,26},{... | collective-permute-start | bytes 706568 | tf_op jit(solution)/shard_map/while/body/eval_jaxpr/ppermute | solution.py:14
  401.0 57.5 %all-to-all-start.1 = ((f32[1,8,8]{2,0,1:T(1,128)}), f32[1,8,8]{2,0,1:T(1,128)S(1)}, u32[]{:S(2)}, u32[]{:S(2)}) async-start(f32[1,8,8]{2,0,1:T(1,128)} %bitcast.2454), calls=%async_computation.1 | async-start | bytes 8192 | tf_op jit(solution)/shard_map/while/body/eval_jaxpr/all_to_all | solution.py:160
  458.5 9.1 %all-to-all-start = ((f32[1,8,8,230]{3,2,0,1:T(8,128)}), f32[1,8,8,230]{3,2,0,1:T(8,128)S(1)}, u32[]{:S(2)}, u32[]{:S(2)}) async-start(f32[1,8,8,230]{3,2,0,1:T(8,128)} %convolution_bitcast_fusion.4), calls=%async_computation | async-start | bytes 131072 | tf_op jit(solution)/shard_map/while/body/eval_jaxpr/all_to_all | solution.py:159
  468.0 0.6 copy-start
  469.4 0.7 slice-start
  471.3 0.7 copy-start.1
  473.8 19.7 %collective-permute-start = (f32[1,230,256]{2,1,0:T(8,128)S(1)}, f32[1,230,256]{2,1,0:T(8,128)S(1)}, u32[]{:S(2)}, u32[]{:S(2)}) collective-permute-start(f32[1,230,256]{2,1,0:T(8,128)S(1)} %pad_maximum_fusion.2), channel_id=1, source_target_pairs={{0,8},{8,16},{16,24},{1,9},{9,17},{17,25},{2,10},{10,18},{18,26},{... | collective-permute-start | bytes 706568 | tf_op jit(solution)/shard_map/while/body/eval_jaxpr/ppermute | solution.py:14
  498.1 57.7 %all-to-all-start.1 = ((f32[1,8,8]{2,0,1:T(1,128)}), f32[1,8,8]{2,0,1:T(1,128)S(1)}, u32[]{:S(2)}, u32[]{:S(2)}) async-start(f32[1,8,8]{2,0,1:T(1,128)} %bitcast.2454), calls=%async_computation.1 | async-start | bytes 8192 | tf_op jit(solution)/shard_map/while/body/eval_jaxpr/all_to_all | solution.py:160
  555.8 9.1 %all-to-all-start = ((f32[1,8,8,230]{3,2,0,1:T(8,128)}), f32[1,8,8,230]{3,2,0,1:T(8,128)S(1)}, u32[]{:S(2)}, u32[]{:S(2)}) async-start(f32[1,8,8,230]{3,2,0,1:T(8,128)} %convolution_bitcast_fusion.4), calls=%async_computation | async-start | bytes 131072 | tf_op jit(solution)/shard_map/while/body/eval_jaxpr/all_to_all | solution.py:159
  565.2 0.6 copy-start
  566.6 0.7 slice-start
  568.5 0.7 copy-start.1
  571.0 19.5 %collective-permute-start = (f32[1,230,256]{2,1,0:T(8,128)S(1)}, f32[1,230,256]{2,1,0:T(8,128)S(1)}, u32[]{:S(2)}, u32[]{:S(2)}) collective-permute-start(f32[1,230,256]{2,1,0:T(8,128)S(1)} %pad_maximum_fusion.2), channel_id=1, source_target_pairs={{0,8},{8,16},{16,24},{1,9},{9,17},{17,25},{2,10},{10,18},{18,26},{... | collective-permute-start | bytes 706568 | tf_op jit(solution)/shard_map/while/body/eval_jaxpr/ppermute | solution.py:14
  595.1 57.8 %all-to-all-start.1 = ((f32[1,8,8]{2,0,1:T(1,128)}), f32[1,8,8]{2,0,1:T(1,128)S(1)}, u32[]{:S(2)}, u32[]{:S(2)}) async-start(f32[1,8,8]{2,0,1:T(1,128)} %bitcast.2454), calls=%async_computation.1 | async-start | bytes 8192 | tf_op jit(solution)/shard_map/while/body/eval_jaxpr/all_to_all | solution.py:160
  652.9 9.1 %all-to-all-start = ((f32[1,8,8,230]{3,2,0,1:T(8,128)}), f32[1,8,8,230]{3,2,0,1:T(8,128)S(1)}, u32[]{:S(2)}, u32[]{:S(2)}) async-start(f32[1,8,8,230]{3,2,0,1:T(8,128)} %convolution_bitcast_fusion.4), calls=%async_computation | async-start | bytes 131072 | tf_op jit(solution)/shard_map/while/body/eval_jaxpr/all_to_all | solution.py:159
  662.4 0.6 copy-start
  663.8 0.7 slice-start
  665.7 0.7 copy-start.1
  668.2 19.4 %collective-permute-start = (f32[1,230,256]{2,1,0:T(8,128)S(1)}, f32[1,230,256]{2,1,0:T(8,128)S(1)}, u32[]{:S(2)}, u32[]{:S(2)}) collective-permute-start(f32[1,230,256]{2,1,0:T(8,128)S(1)} %pad_maximum_fusion.2), channel_id=1, source_target_pairs={{0,8},{8,16},{16,24},{1,9},{9,17},{17,25},{2,10},{10,18},{18,26},{... | collective-permute-start | bytes 706568 | tf_op jit(solution)/shard_map/while/body/eval_jaxpr/ppermute | solution.py:14
  687.6 0.9 copy-start.2
  687.6 0.9 copy-start.3
where the time goes:
time: 692 us; the launch traced here: 689 us
  blocking collectives  296 us (43%)
  starting transfers between devices  145 us (21%)
  local copies, waits for them, and re-layouts  109 us (16%)
  other arithmetic  68.2 us (10%)
  waiting for transfers between devices  30.8 us (4%)
  loops' own time  25.7 us (4%)
  matrix products  12.9 us (2%)
    all_gather x7, blocking collectives, window_work(): all_coeffs = lax.all_gather(beta_prior, 'obs', axis=2, tiled=True)  173 us
    psum x7, blocking collectives, window_work(): totals = lax.psum(statistics, 'obs')  123 us
    ppermute x7, starting transfers between devices, from_behind(): return lax.ppermute(array, axis, pairs)  95 us
    dynamic_update_slice x28, local copies, waits for them, and re-layouts, store_entry(): return lax.dynamic_update_slice_in_dim(buffer, updated, slot_index, 1)  43.8 us
    all_to_all x7, waiting for transfers between devices, window_work(): lax.all_to_all(send_rows, 'obs', split_axis=1, concat_axis=1, tiled=True)  30.8 us
    all_to_all x7, starting transfers between devices, window_work(): lax.all_to_all(send_channel, 'obs', split_axis=1, concat_axis=1, tiled=True)  26.2 us
    another operation x1, loops' own time, local(): lax.fori_loop(0, stream_count + section_count - 1, tick_step, initial)  25.7 us
    all_to_all x7, starting transfers between devices, window_work(): lax.all_to_all(send_rows, 'obs', split_axis=1, concat_axis=1, tiled=True)  23.5 us
  transfers between devices with their start and end apart: 21, of which 7 were waited for; matrix products, arithmetic and copies ran while one was open for 18% of the time, Pallas kernels for 0%

commit v1 on v0

--- a/solution.py
+++ b/solution.py
@@ -141,7 +141,14 @@
     def window_work(state_now, streams):
         beta_prior = state_now[:, :pred_count]
         info_prior = state_now[:, pred_count:]
-        all_coeffs = lax.all_gather(beta_prior, "obs", axis=2, tiled=True)
+        ring = [beta_prior]
+        for hop in range(7):
+            ring.append(lax.ppermute(ring[-1], "obs", [(dev, (dev + 1) % 8) for dev in range(8)]))
+        all_coeffs = jnp.roll(
+            jnp.concatenate(ring[::-1], axis=2),
+            (lax.axis_index("obs") + 1) * ring[0].shape[2],
+            axis=2,
+        )
         channel = jnp.take(block_channel[0], streams, axis=0)
         block_coeffs = jax.vmap(lambda coeff_rows, chan: jnp.take(coeff_rows, chan, axis=1))(
             all_coeffs, channel

time: 692 us -> 729 us (1.053)
  waiting for transfers between devices: 30.8 us -> 205 us
  blocking collectives: 296 us -> 124 us
  starting transfers between devices: 145 us -> 168 us
  other arithmetic: 68.2 us -> 75.6 us
    ppermute x0 -> x49, waiting for transfers between devices: none -> 205 us  [window_work(): lax.ppermute(ring[-1], 'obs', [(dev, (dev + 1) % 8) for dev in range(8)])]
    all_gather x7 -> x0, blocking collectives: 173 us -> none  [window_work(): all_coeffs = lax.all_gather(beta_prior, 'obs', axis=2, tiled=True)]
    all_to_all x7, waiting for transfers between devices: 30.8 us -> 0.02 us  [window_work(): lax.all_to_all(send_rows, 'obs', split_axis=1, concat_axis=1, tiled=True)]
    ppermute x0 -> x49, starting transfers between devices: none -> 13.1 us  [window_work(): lax.ppermute(ring[-1], 'obs', [(dev, (dev + 1) % 8) for dev in range(8)])]
    all_to_all x7, starting transfers between devices: 26.2 us -> 37.1 us  [window_work(): lax.all_to_all(send_channel, 'obs', split_axis=1, concat_axis=1, tiled=True)]
  transfers between devices with their start and end apart: 21 -> 70, of which waited for: 7 -> 42; matrix products, arithmetic and copies ran while one was open for 18% -> 11% of each run, Pallas kernels for 0% -> 0%
where the time goes in v1:
time: 729 us; the launch traced here: 726 us
  waiting for transfers between devices  205 us (28%)
  starting transfers between devices  168 us (23%)
  blocking collectives  124 us (17%)
  local copies, waits for them, and re-layouts  112 us (15%)
  other arithmetic  75.6 us (10%)
  loops' own time  27.5 us (4%)
  matrix products  12.9 us (2%)
    ppermute x49, waiting for transfers between devices, window_work(): lax.ppermute(ring[-1], 'obs', [(dev, (dev + 1) % 8) for dev in range(8)])  205 us
    psum x7, blocking collectives, window_work(): totals = lax.psum(statistics, 'obs')  124 us
    ppermute x7, starting transfers between devices, from_behind(): return lax.ppermute(array, axis, pairs)  94.1 us
    dynamic_update_slice x28, local copies, waits for them, and re-layouts, store_entry(): return lax.dynamic_update_slice_in_dim(buffer, updated, slot_index, 1)  43.8 us
    all_to_all x7, starting transfers between devices, window_work(): lax.all_to_all(send_channel, 'obs', split_axis=1, concat_axis=1, tiled=True)  37.1 us
    another operation x1, loops' own time, local(): lax.fori_loop(0, stream_count + section_count - 1, tick_step, initial)  27.5 us
    all_to_all x7, starting transfers between devices, window_work(): lax.all_to_all(send_rows, 'obs', split_axis=1, concat_axis=1, tiled=True)  23.5 us
  transfers between devices with their start and end apart: 70, of which 42 were waited for; matrix products, arithmetic and copies ran while one was open for 11% of the time, Pallas kernels for 0%

profile of v1, /device:TPU:1, one launch (start us, length us, event | category | flops | bytes accessed | tf_op | source)
XLA Modules:
  0.0 725.5 jit_solution(1649067539002671932)
XLA Ops:
  3.8 720.8 %while.38 = (s32[]{:T(128)}, f32[1,230,256]{2,1,0:T(8,128)S(1)}, f32[1,4,20,256]{3,1,2,0:T(4,128)S(1)}, f32[1,4,210,256]{3,1,2,0:T(4,128)S(1)}, s32[]{:T(128)}, ...) while((s32[]{:T(128)}, f32[1,230,256]{2,1,0:T(8,128)S(1)}, ...), condition=%wide.region_8.10_spmd.clone.clone, body=%wide.region_0.9_spmd.sunk.clone.clone.sunk | while | flops 57759528 | bytes 22234704 | solution.py:206
  13.0 4.6 all-to-all-start.1
  24.0 5.4 collective-permute-done.2
  29.4 5.4 collective-permute-done.3
  34.9 5.2 collective-permute-done.4
  40.1 5.4 collective-permute-done.5
  47.0 3.9 collective-permute-done.6
  62.0 17.7 %psum.19 = f32[1,2]{1,0:T(1,128)S(1)} all-reduce(f32[1,2]{1,0:T(1,128)S(1)} %maximum_bitcast_fusion.6), channel_id=1, replica_groups=mesh['section'=4,'obs'=8] {'obs'}, use_global_device_ids=true, to_apply=%region_7.8 | all-reduce | flops 2 | bytes 16 | tf_op jit(solution)/shard_map/while/body/eval_jaxpr/psum | solution.py:163
  87.9 15.1 %collective-permute-start.7 = (f32[1,230,256]{2,1,0:T(8,128)S(1)}, f32[1,230,256]{2,1,0:T(8,128)S(1)}, u32[]{:S(2)}, u32[]{:S(2)}) collective-permute-start(f32[1,230,256]{2,1,0:T(8,128)S(1)} %pad_maximum_fusion.2), channel_id=1, source_target_pairs={{0,8},{8,16},{16,24},{1,9},{9,17},{17,25},{2,10},{10,18},{18,26},{... | collective-permute-start | bytes 706568 | tf_op jit(solution)/shard_map/while/body/eval_jaxpr/ppermute | solution.py:14
  103.4 5.9 dynamic_update_slice.31
  116.5 5.4 all-to-all-start.1
  128.3 5.4 collective-permute-done.2
  133.7 5.4 collective-permute-done.3
  139.3 5.2 collective-permute-done.4
  144.5 5.3 collective-permute-done.5
  151.3 3.9 collective-permute-done.6
  166.3 17.8 %psum.19 = f32[1,2]{1,0:T(1,128)S(1)} all-reduce(f32[1,2]{1,0:T(1,128)S(1)} %maximum_bitcast_fusion.6), channel_id=1, replica_groups=mesh['section'=4,'obs'=8] {'obs'}, use_global_device_ids=true, to_apply=%region_7.8 | all-reduce | flops 2 | bytes 16 | tf_op jit(solution)/shard_map/while/body/eval_jaxpr/psum | solution.py:163
  192.2 13.4 %collective-permute-start.7 = (f32[1,230,256]{2,1,0:T(8,128)S(1)}, f32[1,230,256]{2,1,0:T(8,128)S(1)}, u32[]{:S(2)}, u32[]{:S(2)}) collective-permute-start(f32[1,230,256]{2,1,0:T(8,128)S(1)} %pad_maximum_fusion.2), channel_id=1, source_target_pairs={{0,8},{8,16},{16,24},{1,9},{9,17},{17,25},{2,10},{10,18},{18,26},{... | collective-permute-start | bytes 706568 | tf_op jit(solution)/shard_map/while/body/eval_jaxpr/ppermute | solution.py:14
  205.9 5.9 dynamic_update_slice.31
  219.0 5.4 all-to-all-start.1
  230.9 5.6 collective-permute-done.2
  236.5 5.4 collective-permute-done.3
  242.1 5.2 collective-permute-done.4
  247.3 5.3 collective-permute-done.5
  254.1 3.9 collective-permute-done.6
  269.1 18.1 %psum.19 = f32[1,2]{1,0:T(1,128)S(1)} all-reduce(f32[1,2]{1,0:T(1,128)S(1)} %maximum_bitcast_fusion.6), channel_id=1, replica_groups=mesh['section'=4,'obs'=8] {'obs'}, use_global_device_ids=true, to_apply=%region_7.8 | all-reduce | flops 2 | bytes 16 | tf_op jit(solution)/shard_map/while/body/eval_jaxpr/psum | solution.py:163
  295.3 12.8 %collective-permute-start.7 = (f32[1,230,256]{2,1,0:T(8,128)S(1)}, f32[1,230,256]{2,1,0:T(8,128)S(1)}, u32[]{:S(2)}, u32[]{:S(2)}) collective-permute-start(f32[1,230,256]{2,1,0:T(8,128)S(1)} %pad_maximum_fusion.2), channel_id=1, source_target_pairs={{0,8},{8,16},{16,24},{1,9},{9,17},{17,25},{2,10},{10,18},{18,26},{... | collective-permute-start | bytes 706568 | tf_op jit(solution)/shard_map/while/body/eval_jaxpr/ppermute | solution.py:14
  308.5 5.9 dynamic_update_slice.31
  321.6 5.4 all-to-all-start.1
  333.4 5.4 collective-permute-done.2
  338.8 5.4 collective-permute-done.3
  344.3 5.2 collective-permute-done.4
  349.6 5.3 collective-permute-done.5
  356.3 3.9 collective-permute-done.6
  371.4 17.8 %psum.19 = f32[1,2]{1,0:T(1,128)S(1)} all-reduce(f32[1,2]{1,0:T(1,128)S(1)} %maximum_bitcast_fusion.6), channel_id=1, replica_groups=mesh['section'=4,'obs'=8] {'obs'}, use_global_device_ids=true, to_apply=%region_7.8 | all-reduce | flops 2 | bytes 16 | tf_op jit(solution)/shard_map/while/body/eval_jaxpr/psum | solution.py:163
  397.2 13.4 %collective-permute-start.7 = (f32[1,230,256]{2,1,0:T(8,128)S(1)}, f32[1,230,256]{2,1,0:T(8,128)S(1)}, u32[]{:S(2)}, u32[]{:S(2)}) collective-permute-start(f32[1,230,256]{2,1,0:T(8,128)S(1)} %pad_maximum_fusion.2), channel_id=1, source_target_pairs={{0,8},{8,16},{16,24},{1,9},{9,17},{17,25},{2,10},{10,18},{18,26},{... | collective-permute-start | bytes 706568 | tf_op jit(solution)/shard_map/while/body/eval_jaxpr/ppermute | solution.py:14
  411.0 5.9 dynamic_update_slice.31
  424.1 5.4 all-to-all-start.1
  436.0 5.4 collective-permute-done.2
  441.3 5.7 collective-permute-done.3
  447.2 5.2 collective-permute-done.4
  452.4 5.3 collective-permute-done.5
  459.2 3.9 collective-permute-done.6
  474.2 17.7 %psum.19 = f32[1,2]{1,0:T(1,128)S(1)} all-reduce(f32[1,2]{1,0:T(1,128)S(1)} %maximum_bitcast_fusion.6), channel_id=1, replica_groups=mesh['section'=4,'obs'=8] {'obs'}, use_global_device_ids=true, to_apply=%region_7.8 | all-reduce | flops 2 | bytes 16 | tf_op jit(solution)/shard_map/while/body/eval_jaxpr/psum | solution.py:163
  500.1 13.1 %collective-permute-start.7 = (f32[1,230,256]{2,1,0:T(8,128)S(1)}, f32[1,230,256]{2,1,0:T(8,128)S(1)}, u32[]{:S(2)}, u32[]{:S(2)}) collective-permute-start(f32[1,230,256]{2,1,0:T(8,128)S(1)} %pad_maximum_fusion.2), channel_id=1, source_target_pairs={{0,8},{8,16},{16,24},{1,9},{9,17},{17,25},{2,10},{10,18},{18,26},{... | collective-permute-start | bytes 706568 | tf_op jit(solution)/shard_map/while/body/eval_jaxpr/ppermute | solution.py:14
  513.6 5.9 dynamic_update_slice.31
  526.7 5.4 all-to-all-start.1
  538.5 5.4 collective-permute-done.2
  543.9 5.4 collective-permute-done.3
  549.4 5.2 collective-permute-done.4
  554.6 5.3 collective-permute-done.5
  561.4 3.9 collective-permute-done.6
  576.5 17.7 %psum.19 = f32[1,2]{1,0:T(1,128)S(1)} all-reduce(f32[1,2]{1,0:T(1,128)S(1)} %maximum_bitcast_fusion.6), channel_id=1, replica_groups=mesh['section'=4,'obs'=8] {'obs'}, use_global_device_ids=true, to_apply=%region_7.8 | all-reduce | flops 2 | bytes 16 | tf_op jit(solution)/shard_map/while/body/eval_jaxpr/psum | solution.py:163
  602.3 13.4 %collective-permute-start.7 = (f32[1,230,256]{2,1,0:T(8,128)S(1)}, f32[1,230,256]{2,1,0:T(8,128)S(1)}, u32[]{:S(2)}, u32[]{:S(2)}) collective-permute-start(f32[1,230,256]{2,1,0:T(8,128)S(1)} %pad_maximum_fusion.2), channel_id=1, source_target_pairs={{0,8},{8,16},{16,24},{1,9},{9,17},{17,25},{2,10},{10,18},{18,26},{... | collective-permute-start | bytes 706568 | tf_op jit(solution)/shard_map/while/body/eval_jaxpr/ppermute | solution.py:14
  616.1 5.9 dynamic_update_slice.31
  629.2 5.4 all-to-all-start.1
  641.0 5.4 collective-permute-done.2
  646.4 5.4 collective-permute-done.3
  652.0 5.6 collective-permute-done.4
  657.6 5.3 collective-permute-done.5
  664.4 3.9 collective-permute-done.6
  679.5 17.7 %psum.19 = f32[1,2]{1,0:T(1,128)S(1)} all-reduce(f32[1,2]{1,0:T(1,128)S(1)} %maximum_bitcast_fusion.6), channel_id=1, replica_groups=mesh['section'=4,'obs'=8] {'obs'}, use_global_device_ids=true, to_apply=%region_7.8 | all-reduce | flops 2 | bytes 16 | tf_op jit(solution)/shard_map/while/body/eval_jaxpr/psum | solution.py:163
  705.3 13.0 %collective-permute-start.7 = (f32[1,230,256]{2,1,0:T(8,128)S(1)}, f32[1,230,256]{2,1,0:T(8,128)S(1)}, u32[]{:S(2)}, u32[]{:S(2)}) collective-permute-start(f32[1,230,256]{2,1,0:T(8,128)S(1)} %pad_maximum_fusion.2), channel_id=1, source_target_pairs={{0,8},{8,16},{16,24},{1,9},{9,17},{17,25},{2,10},{10,18},{18,26},{... | collective-permute-start | bytes 706568 | tf_op jit(solution)/shard_map/while/body/eval_jaxpr/ppermute | solution.py:14
  718.6 5.9 dynamic_update_slice.31
  (854 shorter events, 222.9 us)
Async XLA Ops:
  8.8 9.7 %collective-permute-start = (f32[1,20,256]{2,1,0:T(8,128)S(1)}, f32[1,20,256]{2,1,0:T(8,128)S(1)}, u32[]{:S(2)}, u32[]{:S(2)}) collective-permute-start(f32[1,20,256]{2,1,0:T(8,128)S(1)} %slice.5348), channel_id=1, source_target_pairs={{0,1},{1,2},{2,3},{3,4},{4,5},{5,6},{6,7},{7,0},{8,9},{9,10},{10,1... | collective-permute-start | bytes 61448 | tf_op jit(solution)/shard_map/while/body/eval_jaxpr/ppermute | solution.py:146
  13.0 32.8 %all-to-all-start.1 = ((f32[1,8,8]{2,0,1:T(1,128)}), f32[1,8,8]{2,0,1:T(1,128)S(1)}, u32[]{:S(2)}, u32[]{:S(2)}) async-start(f32[1,8,8]{2,0,1:T(1,128)} %bitcast.2454), calls=%async_computation.1 | async-start | bytes 8192 | tf_op jit(solution)/shard_map/while/body/eval_jaxpr/all_to_all | solution.py:167
  18.6 5.4 collective-permute-start.1
  24.0 5.4 collective-permute-start.2
  29.4 5.4 collective-permute-start.3
  34.7 5.4 collective-permute-start.4
  40.1 5.5 collective-permute-start.5
  45.6 5.4 collective-permute-start.6
  58.7 23.0 %all-to-all-start = ((f32[1,8,8,230]{3,2,0,1:T(8,128)}), f32[1,8,8,230]{3,2,0,1:T(8,128)S(1)}, u32[]{:S(2)}, u32[]{:S(2)}) async-start(f32[1,8,8,230]{3,2,0,1:T(8,128)} %convolution_bitcast_fusion.4), calls=%async_computation | async-start | bytes 131072 | tf_op jit(solution)/shard_map/while/body/eval_jaxpr/all_to_all | solution.py:166
  87.9 21.4 %collective-permute-start.7 = (f32[1,230,256]{2,1,0:T(8,128)S(1)}, f32[1,230,256]{2,1,0:T(8,128)S(1)}, u32[]{:S(2)}, u32[]{:S(2)}) collective-permute-start(f32[1,230,256]{2,1,0:T(8,128)S(1)} %pad_maximum_fusion.2), channel_id=1, source_target_pairs={{0,8},{8,16},{16,24},{1,9},{9,17},{17,25},{2,10},{10,18},{18,26},{... | collective-permute-start | bytes 706568 | tf_op jit(solution)/shard_map/while/body/eval_jaxpr/ppermute | solution.py:14
  114.4 8.5 %collective-permute-start = (f32[1,20,256]{2,1,0:T(8,128)S(1)}, f32[1,20,256]{2,1,0:T(8,128)S(1)}, u32[]{:S(2)}, u32[]{:S(2)}) collective-permute-start(f32[1,20,256]{2,1,0:T(8,128)S(1)} %slice.5348), channel_id=1, source_target_pairs={{0,1},{1,2},{2,3},{3,4},{4,5},{5,6},{6,7},{7,0},{8,9},{9,10},{10,1... | collective-permute-start | bytes 61448 | tf_op jit(solution)/shard_map/while/body/eval_jaxpr/ppermute | solution.py:146
  116.5 33.5 %all-to-all-start.1 = ((f32[1,8,8]{2,0,1:T(1,128)}), f32[1,8,8]{2,0,1:T(1,128)S(1)}, u32[]{:S(2)}, u32[]{:S(2)}) async-start(f32[1,8,8]{2,0,1:T(1,128)} %bitcast.2454), calls=%async_computation.1 | async-start | bytes 8192 | tf_op jit(solution)/shard_map/while/body/eval_jaxpr/all_to_all | solution.py:167
  122.9 5.4 collective-permute-start.1
  128.3 5.4 collective-permute-start.2
  133.7 5.4 collective-permute-start.3
  139.1 5.4 collective-permute-start.4
  144.4 5.4 collective-permute-start.5
  149.8 5.4 collective-permute-start.6
  162.9 23.0 %all-to-all-start = ((f32[1,8,8,230]{3,2,0,1:T(8,128)}), f32[1,8,8,230]{3,2,0,1:T(8,128)S(1)}, u32[]{:S(2)}, u32[]{:S(2)}) async-start(f32[1,8,8,230]{3,2,0,1:T(8,128)} %convolution_bitcast_fusion.4), calls=%async_computation | async-start | bytes 131072 | tf_op jit(solution)/shard_map/while/body/eval_jaxpr/all_to_all | solution.py:166
  192.2 19.7 %collective-permute-start.7 = (f32[1,230,256]{2,1,0:T(8,128)S(1)}, f32[1,230,256]{2,1,0:T(8,128)S(1)}, u32[]{:S(2)}, u32[]{:S(2)}) collective-permute-start(f32[1,230,256]{2,1,0:T(8,128)S(1)} %pad_maximum_fusion.2), channel_id=1, source_target_pairs={{0,8},{8,16},{16,24},{1,9},{9,17},{17,25},{2,10},{10,18},{18,26},{... | collective-permute-start | bytes 706568 | tf_op jit(solution)/shard_map/while/body/eval_jaxpr/ppermute | solution.py:14
  216.9 8.5 %collective-permute-start = (f32[1,20,256]{2,1,0:T(8,128)S(1)}, f32[1,20,256]{2,1,0:T(8,128)S(1)}, u32[]{:S(2)}, u32[]{:S(2)}) collective-permute-start(f32[1,20,256]{2,1,0:T(8,128)S(1)} %slice.5348), channel_id=1, source_target_pairs={{0,1},{1,2},{2,3},{3,4},{4,5},{5,6},{6,7},{7,0},{8,9},{9,10},{10,1... | collective-permute-start | bytes 61448 | tf_op jit(solution)/shard_map/while/body/eval_jaxpr/ppermute | solution.py:146
  219.0 33.8 %all-to-all-start.1 = ((f32[1,8,8]{2,0,1:T(1,128)}), f32[1,8,8]{2,0,1:T(1,128)S(1)}, u32[]{:S(2)}, u32[]{:S(2)}) async-start(f32[1,8,8]{2,0,1:T(1,128)} %bitcast.2454), calls=%async_computation.1 | async-start | bytes 8192 | tf_op jit(solution)/shard_map/while/body/eval_jaxpr/all_to_all | solution.py:167
  225.4 5.4 collective-permute-start.1
  230.9 5.6 collective-permute-start.2
  236.5 5.4 collective-permute-start.3
  241.9 5.4 collective-permute-start.4
  247.3 5.4 collective-permute-start.5
  252.6 5.4 collective-permute-start.6
  265.7 23.3 %all-to-all-start = ((f32[1,8,8,230]{3,2,0,1:T(8,128)}), f32[1,8,8,230]{3,2,0,1:T(8,128)S(1)}, u32[]{:S(2)}, u32[]{:S(2)}) async-start(f32[1,8,8,230]{3,2,0,1:T(8,128)} %convolution_bitcast_fusion.4), calls=%async_computation | async-start | bytes 131072 | tf_op jit(solution)/shard_map/while/body/eval_jaxpr/all_to_all | solution.py:166
  295.3 19.1 %collective-permute-start.7 = (f32[1,230,256]{2,1,0:T(8,128)S(1)}, f32[1,230,256]{2,1,0:T(8,128)S(1)}, u32[]{:S(2)}, u32[]{:S(2)}) collective-permute-start(f32[1,230,256]{2,1,0:T(8,128)S(1)} %pad_maximum_fusion.2), channel_id=1, source_target_pairs={{0,8},{8,16},{16,24},{1,9},{9,17},{17,25},{2,10},{10,18},{18,26},{... | collective-permute-start | bytes 706568 | tf_op jit(solution)/shard_map/while/body/eval_jaxpr/ppermute | solution.py:14
  319.5 8.5 %collective-permute-start = (f32[1,20,256]{2,1,0:T(8,128)S(1)}, f32[1,20,256]{2,1,0:T(8,128)S(1)}, u32[]{:S(2)}, u32[]{:S(2)}) collective-permute-start(f32[1,20,256]{2,1,0:T(8,128)S(1)} %slice.5348), channel_id=1, source_target_pairs={{0,1},{1,2},{2,3},{3,4},{4,5},{5,6},{6,7},{7,0},{8,9},{9,10},{10,1... | collective-permute-start | bytes 61448 | tf_op jit(solution)/shard_map/while/body/eval_jaxpr/ppermute | solution.py:146
  321.6 33.5 %all-to-all-start.1 = ((f32[1,8,8]{2,0,1:T(1,128)}), f32[1,8,8]{2,0,1:T(1,128)S(1)}, u32[]{:S(2)}, u32[]{:S(2)}) async-start(f32[1,8,8]{2,0,1:T(1,128)} %bitcast.2454), calls=%async_computation.1 | async-start | bytes 8192 | tf_op jit(solution)/shard_map/while/body/eval_jaxpr/all_to_all | solution.py:167
  328.0 5.4 collective-permute-start.1
  333.4 5.4 collective-permute-start.2
  338.8 5.4 collective-permute-start.3
  344.2 5.4 collective-permute-start.4
  349.5 5.4 collective-permute-start.5
  354.9 5.4 collective-permute-start.6
  368.0 23.0 %all-to-all-start = ((f32[1,8,8,230]{3,2,0,1:T(8,128)}), f32[1,8,8,230]{3,2,0,1:T(8,128)S(1)}, u32[]{:S(2)}, u32[]{:S(2)}) async-start(f32[1,8,8,230]{3,2,0,1:T(8,128)} %convolution_bitcast_fusion.4), calls=%async_computation | async-start | bytes 131072 | tf_op jit(solution)/shard_map/while/body/eval_jaxpr/all_to_all | solution.py:166
  397.2 19.7 %collective-permute-start.7 = (f32[1,230,256]{2,1,0:T(8,128)S(1)}, f32[1,230,256]{2,1,0:T(8,128)S(1)}, u32[]{:S(2)}, u32[]{:S(2)}) collective-permute-start(f32[1,230,256]{2,1,0:T(8,128)S(1)} %pad_maximum_fusion.2), channel_id=1, source_target_pairs={{0,8},{8,16},{16,24},{1,9},{9,17},{17,25},{2,10},{10,18},{18,26},{... | collective-permute-start | bytes 706568 | tf_op jit(solution)/shard_map/while/body/eval_jaxpr/ppermute | solution.py:14
  422.0 8.5 %collective-permute-start = (f32[1,20,256]{2,1,0:T(8,128)S(1)}, f32[1,20,256]{2,1,0:T(8,128)S(1)}, u32[]{:S(2)}, u32[]{:S(2)}) collective-permute-start(f32[1,20,256]{2,1,0:T(8,128)S(1)} %slice.5348), channel_id=1, source_target_pairs={{0,1},{1,2},{2,3},{3,4},{4,5},{5,6},{6,7},{7,0},{8,9},{9,10},{10,1... | collective-permute-start | bytes 61448 | tf_op jit(solution)/shard_map/while/body/eval_jaxpr/ppermute | solution.py:146
  424.1 33.8 %all-to-all-start.1 = ((f32[1,8,8]{2,0,1:T(1,128)}), f32[1,8,8]{2,0,1:T(1,128)S(1)}, u32[]{:S(2)}, u32[]{:S(2)}) async-start(f32[1,8,8]{2,0,1:T(1,128)} %bitcast.2454), calls=%async_computation.1 | async-start | bytes 8192 | tf_op jit(solution)/shard_map/while/body/eval_jaxpr/all_to_all | solution.py:167
  430.5 5.4 collective-permute-start.1
  435.9 5.4 collective-permute-start.2
  441.3 5.7 collective-permute-start.3
  447.0 5.4 collective-permute-start.4
  470.9 23.0 %all-to-all-start = ((f32[1,8,8,230]{3,2,0,1:T(8,128)}), f32[1,8,8,230]{3,2,0,1:T(8,128)S(1)}, u32[]{:S(2)}, u32[]{:S(2)}) async-start(f32[1,8,8,230]{3,2,0,1:T(8,128)} %convolution_bitcast_fusion.4), calls=%async_computation | async-start | bytes 131072 | tf_op jit(solution)/shard_map/while/body/eval_jaxpr/all_to_all | solution.py:166
  500.1 19.4 %collective-permute-start.7 = (f32[1,230,256]{2,1,0:T(8,128)S(1)}, f32[1,230,256]{2,1,0:T(8,128)S(1)}, u32[]{:S(2)}, u32[]{:S(2)}) collective-permute-start(f32[1,230,256]{2,1,0:T(8,128)S(1)} %pad_maximum_fusion.2), channel_id=1, source_target_pairs={{0,8},{8,16},{16,24},{1,9},{9,17},{17,25},{2,10},{10,18},{18,26},{... | collective-permute-start | bytes 706568 | tf_op jit(solution)/shard_map/while/body/eval_jaxpr/ppermute | solution.py:14
  524.5 8.5 %collective-permute-start = (f32[1,20,256]{2,1,0:T(8,128)S(1)}, f32[1,20,256]{2,1,0:T(8,128)S(1)}, u32[]{:S(2)}, u32[]{:S(2)}) collective-permute-start(f32[1,20,256]{2,1,0:T(8,128)S(1)} %slice.5348), channel_id=1, source_target_pairs={{0,1},{1,2},{2,3},{3,4},{4,5},{5,6},{6,7},{7,0},{8,9},{9,10},{10,1... | collective-permute-start | bytes 61448 | tf_op jit(solution)/shard_map/while/body/eval_jaxpr/ppermute | solution.py:146
  526.7 33.5 %all-to-all-start.1 = ((f32[1,8,8]{2,0,1:T(1,128)}), f32[1,8,8]{2,0,1:T(1,128)S(1)}, u32[]{:S(2)}, u32[]{:S(2)}) async-start(f32[1,8,8]{2,0,1:T(1,128)} %bitcast.2454), calls=%async_computation.1 | async-start | bytes 8192 | tf_op jit(solution)/shard_map/while/body/eval_jaxpr/all_to_all | solution.py:167
  533.1 5.4 collective-permute-start.1
  543.9 5.4 collective-permute-start.3
  549.2 5.4 collective-permute-start.4
  554.6 5.4 collective-permute-start.5
  573.1 23.0 %all-to-all-start = ((f32[1,8,8,230]{3,2,0,1:T(8,128)}), f32[1,8,8,230]{3,2,0,1:T(8,128)S(1)}, u32[]{:S(2)}, u32[]{:S(2)}) async-start(f32[1,8,8,230]{3,2,0,1:T(8,128)} %convolution_bitcast_fusion.4), calls=%async_computation | async-start | bytes 131072 | tf_op jit(solution)/shard_map/while/body/eval_jaxpr/all_to_all | solution.py:166
  602.3 19.7 %collective-permute-start.7 = (f32[1,230,256]{2,1,0:T(8,128)S(1)}, f32[1,230,256]{2,1,0:T(8,128)S(1)}, u32[]{:S(2)}, u32[]{:S(2)}) collective-permute-start(f32[1,230,256]{2,1,0:T(8,128)S(1)} %pad_maximum_fusion.2), channel_id=1, source_target_pairs={{0,8},{8,16},{16,24},{1,9},{9,17},{17,25},{2,10},{10,18},{18,26},{... | collective-permute-start | bytes 706568 | tf_op jit(solution)/shard_map/while/body/eval_jaxpr/ppermute | solution.py:14
  627.1 8.5 %collective-permute-start = (f32[1,20,256]{2,1,0:T(8,128)S(1)}, f32[1,20,256]{2,1,0:T(8,128)S(1)}, u32[]{:S(2)}, u32[]{:S(2)}) collective-permute-start(f32[1,20,256]{2,1,0:T(8,128)S(1)} %slice.5348), channel_id=1, source_target_pairs={{0,1},{1,2},{2,3},{3,4},{4,5},{5,6},{6,7},{7,0},{8,9},{9,10},{10,1... | collective-permute-start | bytes 61448 | tf_op jit(solution)/shard_map/while/body/eval_jaxpr/ppermute | solution.py:146
  629.2 34.0 %all-to-all-start.1 = ((f32[1,8,8]{2,0,1:T(1,128)}), f32[1,8,8]{2,0,1:T(1,128)S(1)}, u32[]{:S(2)}, u32[]{:S(2)}) async-start(f32[1,8,8]{2,0,1:T(1,128)} %bitcast.2454), calls=%async_computation.1 | async-start | bytes 8192 | tf_op jit(solution)/shard_map/while/body/eval_jaxpr/all_to_all | solution.py:167
  635.6 5.4 collective-permute-start.1
  651.8 5.8 collective-permute-start.4
  657.6 5.4 collective-permute-start.5
  663.0 5.4 collective-permute-start.6
  676.1 23.0 %all-to-all-start = ((f32[1,8,8,230]{3,2,0,1:T(8,128)}), f32[1,8,8,230]{3,2,0,1:T(8,128)S(1)}, u32[]{:S(2)}, u32[]{:S(2)}) async-start(f32[1,8,8,230]{3,2,0,1:T(8,128)} %convolution_bitcast_fusion.4), calls=%async_computation | async-start | bytes 131072 | tf_op jit(solution)/shard_map/while/body/eval_jaxpr/all_to_all | solution.py:166
  705.3 19.3 %collective-permute-start.7 = (f32[1,230,256]{2,1,0:T(8,128)S(1)}, f32[1,230,256]{2,1,0:T(8,128)S(1)}, u32[]{:S(2)}, u32[]{:S(2)}) collective-permute-start(f32[1,230,256]{2,1,0:T(8,128)S(1)} %pad_maximum_fusion.2), channel_id=1, source_target_pairs={{0,8},{8,16},{16,24},{1,9},{9,17},{17,25},{2,10},{10,18},{18,26},{... | collective-permute-start | bytes 706568 | tf_op jit(solution)/shard_map/while/body/eval_jaxpr/ppermute | solution.py:14
  (46 other events, 476.9 us)
